TPU v7x, 256 devices: a whole 4x4x8 slice. The times are simulated.
256 devices in a mesh: seq: 64 (over x, z, core), tp: 4 (over y).
Axes of the slice: x: 4, y: 4, z: 8, core: 2. Of those that a mesh axis runs over, the one named last changes fastest.
Arguments:
- hidden_in: bfloat16 [16384, 1536], P('seq', 'tp'), may hold values from -6 to 6
- w_in_gate: float32 [1536, 3072], P('seq', 'tp'), may hold values from -0.15625 to 0.15625
- w_in_value: float32 [1536, 3072], P('seq', 'tp'), may hold values from -0.15625 to 0.15625
- w_in_shared: float32 [1536, 256], P('seq'), may hold values from -0.15625 to 0.15625
- w_in_step: float32 [1536, 48], P('seq', 'tp'), may hold values from -0.15625 to 0.15625
- conv_value: float32 [4, 3072], P(None, 'tp'), may hold values from -3 to 3
- conv_shared: float32 [4, 256], replicated, may hold values from -3 to 3
- dt_bias: float32 [48], P('tp'), may hold values from -4 to -2
- a_log: float32 [48], P('tp'), may hold values from -8 to 0
- skip_gain: float32 [48], P('tp'), may hold values from 0.6 to 4.8
- norm_gain: float32 [3072], P('tp'), may hold values from 0.1 to 1.9
- w_out: float32 [3072, 1536], P('tp', 'seq'), may hold values from -0.109375 to 0.109375
- prompt_lengths: int32 [8], replicated, may hold values from 1 to 8192, 16384 in all
- row_blocks: int32 [64], replicated, may hold values from 0 to 63, each once
Outputs:
- mixed_out: bfloat16 [16384, 1536], P('seq', 'tp')
Inputs may be any that keep to these rules, and one draw needn't show every extreme that they name: `prompt_lengths`: 8 lengths that sum to 16384, the longest exactly 8192. `row_blocks`: a permutation of the row blocks.
All inputs are finite; a program needn't handle non-finite values.
Results may differ from a plain program's by a relative error of at most 0.02.
Values may be sent and summed in bfloat16 or wider, within the bound.
No kernel may reach another device: no remote copies, remote signals or barrier semaphores. Data moves between devices by JAX's collectives and lax.ppermute only.
A program may use at most 128 MiB of HBM per device.

v0:
```python
import jax
import jax.numpy as jnp
from jax import lax
from jax.sharding import PartitionSpec as P

EPSILON = 1e-05
HIGHEST_PREC = lax.Precision.HIGHEST


def passed_along(block, axis, distance):
    devices = range(lax.axis_size(axis))
    route = [(i - distance, i) for i in devices if i - distance in devices]
    return lax.ppermute(block, axis, route)


def prefix_2(x, axis, combine, identity):
    count, here = (lax.axis_size(axis), lax.axis_index(axis))
    everything = jax.tree.map(
        lambda part, kind: lax.all_gather(part.astype(kind), axis), x, (jnp.bfloat16, jnp.bfloat16)
    )
    start = jax.tree.map(
        lambda part, zero: jnp.broadcast_to(jnp.asarray(zero, part.dtype), part.shape), x, identity
    )

    def turn(k, before):
        reached = k < here
        new = combine(
            before, jax.tree.map(lambda part, own: part[k].astype(own.dtype), everything, x)
        )
        return jax.tree.map(lambda a, b: jnp.where(reached, a, b), new, before)

    return lax.fori_loop(0, count, turn, start)


def segment_of(positions, doc_ends):
    return jnp.sum((positions[:, None] >= doc_ends[None, :]).astype(jnp.int32), axis=1)


def span_parts(values, b_half, c_half, steps_dt, decay_rates, segments, prev_seg):
    length = values.shape[0]
    b_rows = b_half.astype(jnp.float32)
    cumulative = jnp.cumsum(-steps_dt * decay_rates[None, :], axis=0)
    places = jnp.arange(length)
    causal = (places[:, None] >= places[None, :]) & (segments[:, None] == segments[None, :])
    gaps_log = jnp.where(causal[:, :, None], cumulative[:, None, :] - cumulative[None, :, :], 0.0)
    decays_in = jnp.where(causal[:, :, None], jnp.exp(gaps_log), 0.0)
    scores = jnp.dot(c_half, b_half.T, preferred_element_type=jnp.float32)
    weights = scores[:, :, None] * decays_in * steps_dt[None, :, :]
    intra_part = jnp.einsum("ijh,jhp->ihp", weights, values, precision=HIGHEST_PREC)
    carry_in = jnp.where((segments == prev_seg)[:, None], jnp.exp(cumulative), 0.0)
    tail_weight = (
        jnp.where(
            (segments == segments[-1])[:, None], jnp.exp(cumulative[-1][None, :] - cumulative), 0.0
        )
        * steps_dt
    )
    fresh_state = jnp.einsum("jh,jhp,jn->hpn", tail_weight, values, b_rows, precision=HIGHEST_PREC)
    keep_factor = jnp.where(segments[-1] == prev_seg, jnp.exp(cumulative[-1]), 0.0)
    return (intra_part, carry_in, fresh_state, keep_factor)


def combine(earlier, later):
    return (earlier[0] * later[0], later[0][:, None, None] * earlier[1] + later[1])


def on_device(
    hidden_in,
    w_in_gate,
    w_in_value,
    w_in_shared,
    w_in_step,
    conv_value,
    conv_shared,
    dt_bias,
    a_log,
    skip_gain,
    norm_gain,
    w_out,
    prompt_lengths,
    row_blocks,
):
    seq_count = lax.axis_size("seq")
    tokens_here = hidden_in.shape[0]
    edge_count = conv_value.shape[0] - 1
    gathered = lax.all_gather(hidden_in, "tp", axis=1, tiled=True)
    row_count = gathered.shape[0]
    model_width = gathered.shape[1]
    permuted = jnp.take(
        gathered.reshape(row_count, seq_count, model_width // seq_count), row_blocks, axis=1
    ).reshape(row_count, model_width)
    stored = (
        w_in_gate.astype(jnp.bfloat16),
        w_in_value.astype(jnp.bfloat16),
        w_in_shared.astype(jnp.bfloat16),
        w_in_step.astype(jnp.bfloat16),
    )
    pieces = (
        lax.all_gather(stored[0], "seq", axis=0, tiled=True),
        lax.all_gather(stored[1], "seq", axis=0, tiled=True),
        lax.all_gather(stored[2], "seq", axis=0, tiled=True),
        lax.all_gather(stored[3], "seq", axis=0, tiled=True),
    )
    projected = tuple(
        (
            jnp.dot(permuted, weight_piece, preferred_element_type=jnp.float32)
            for weight_piece in pieces
        )
    )
    gate_all, value_all, shared_all, raw_all = [result.astype(jnp.bfloat16) for result in projected]
    mixed_in = jnp.concatenate([value_all, shared_all], axis=1)
    edge_mix = passed_along(mixed_in[tokens_here - edge_count :], "seq", 1)
    doc_ends = jnp.cumsum(prompt_lengths)
    first_pos = lax.axis_index("seq") * tokens_here
    positions = first_pos + jnp.arange(tokens_here, dtype=jnp.int32)
    edge_positions = first_pos - edge_count + jnp.arange(edge_count, dtype=jnp.int32)
    segments = segment_of(positions, doc_ends)
    ext_segments = jnp.concatenate([segment_of(edge_positions, doc_ends), segments])
    ext_rows = jnp.concatenate([edge_mix, mixed_in], axis=0)
    kernel = jnp.concatenate([conv_value, conv_shared], axis=1)
    conv_sum = jnp.zeros(mixed_in.shape, jnp.float32)
    for tap_index in range(edge_count + 1):
        same_doc = (ext_segments[tap_index : tap_index + tokens_here] == segments)[:, None]
        conv_sum = conv_sum + jnp.where(
            same_doc,
            kernel[tap_index][None, :]
            * ext_rows[tap_index : tap_index + tokens_here].astype(jnp.float32),
            0.0,
        )
    convolved = jax.nn.silu(conv_sum).astype(jnp.bfloat16)
    local_inner = conv_value.shape[1]
    local_heads = dt_bias.shape[0]
    head_dim = local_inner // local_heads
    state_size = conv_shared.shape[1] // 2
    values = (
        convolved[:, :local_inner].astype(jnp.float32).reshape(tokens_here, local_heads, head_dim)
    )
    b_half = convolved[:, local_inner : local_inner + state_size]
    c_half = convolved[:, local_inner + state_size :]
    c_rows = c_half.astype(jnp.float32)
    steps_dt = jax.nn.softplus(raw_all.astype(jnp.float32) + dt_bias[None, :])
    decay_rates = jnp.exp(a_log)
    prev_first = segment_of(jnp.reshape(first_pos - 1, (1,)), doc_ends)[0]
    device_keep = jnp.ones((local_heads,), jnp.float32)
    device_state = jnp.zeros((local_heads, head_dim, state_size), jnp.float32)
    parts = span_parts(values, b_half, c_half, steps_dt, decay_rates, segments, prev_first)
    device_keep = parts[3] * device_keep
    device_state = parts[3][:, None, None] * device_state + parts[2]
    identity = (jnp.ones_like(device_keep), jnp.zeros_like(device_state))
    prefix = prefix_2((device_keep, device_state), "seq", combine, identity)
    carried = prefix[1]
    intra_part, carry_in, fresh_state, keep_factor = parts
    inter_part = (
        jnp.einsum("in,hpn->ihp", c_rows, carried, precision=HIGHEST_PREC) * carry_in[:, :, None]
    )
    outputs = intra_part + inter_part
    mixed_heads = outputs + skip_gain[None, :, None] * values
    gated = mixed_heads.reshape(tokens_here, local_inner) * jax.nn.silu(
        gate_all.astype(jnp.float32)
    )
    squares = jnp.sum(gated * gated, axis=1)
    square_total = lax.psum(squares, "tp")
    mean_square = square_total / (local_inner * lax.axis_size("tp"))
    normed = (gated * lax.rsqrt(mean_square + EPSILON)[:, None] * norm_gain[None, :]).astype(
        jnp.bfloat16
    )
    out_weight = w_out.astype(jnp.bfloat16)
    partial_terms = jnp.dot(
        normed,
        lax.all_gather(out_weight, "seq", axis=1, tiled=True),
        preferred_element_type=jnp.float32,
    )
    return lax.psum_scatter(
        partial_terms.astype(jnp.bfloat16), "tp", scatter_dimension=1, tiled=True
    )


def solution(mesh):
    return jax.shard_map(
        on_device,
        mesh=mesh,
        in_specs=(
            P("seq", "tp"),
            P("seq", "tp"),
            P("seq", "tp"),
            P("seq", None),
            P("seq", "tp"),
            P(None, "tp"),
            P(),
            P("tp"),
            P("tp"),
            P("tp"),
            P("tp"),
            P("tp", "seq"),
            P(),
            P(),
        ),
        out_specs=P("seq", "tp"),
        check_vma=False,
    )
```

profile of v0, /device:TPU:2, one launch (start us, length us, event | category | flops | bytes accessed | tf_op | source)
XLA Modules:
  0.0 420.0 jit_solution(3729731392679539498)
XLA Ops:
  6.5 1.5 convert_element_type.112
  13.0 46.7 %all-gather.1 = bf16[64,24,12]{1,2,0:T(8,128)(2,1)S(1)} all-gather(bf16[1,24,12]{1,2,0:T(8,128)(2,1)S(1)} %convert_bitcast_fusion), channel_id=1, replica_groups=mesh['seq'=64,'tp'=4] {'seq'}, dimensions={0}, use_global_device_ids=true | all-gather | bytes 37440 | tf_op jit(solution)/shard_map/all_gather | solution.py:101
  61.4 14.2 %all_gather.28 = bf16[256,1536]{0,1:T(8,128)(2,1)S(1)} all-gather(bf16[256,384]{0,1:T(8,128)(2,1)S(1)} %copy.39), channel_id=1, replica_groups=mesh['seq'=64,'tp'=4] {'tp'}, dimensions={1}, use_global_device_ids=true | all-gather | bytes 983040 | tf_op jit(solution)/shard_map/all_gather | solution.py:85
  80.0 48.3 %all_gather.30 = bf16[1536,256]{1,0:T(8,128)(2,1)S(1)} all-gather(bf16[24,256]{1,0:T(8,128)(2,1)S(1)} %convert_element_type.114), channel_id=1, replica_groups=mesh['seq'=64,'tp'=4] {'seq'}, dimensions={0}, use_global_device_ids=true | all-gather | bytes 798720 | tf_op jit(solution)/shard_map/all_gather | solution.py:100
  128.3 1.3 broadcast_compare_fusion
  130.1 2.5 convolution_convert_fusion.2
  132.6 2.3 collective-permute-start
  134.9 4.8 %collective-permute-done = bf16[3,1024]{1,0:T(4,128)(2,1)S(1)} collective-permute-done((bf16[3,1024]{1,0:T(4,128)(2,1)S(1)}, bf16[3,1024]{1,0:T(4,128)(2,1)S(1)}, u32[]{:S(2)}, u32[]{:S(2)}) %collective-permute-start) | collective-permute-done | bytes 6176 | tf_op jit(solution)/shard_map/ppermute | solution.py:13
  140.9 1.2 fusion.20
  143.9 38.1 %all-gather.2 = bf16[64,1,12]{2,1,0:T(2,128)(2,1)S(1)} all-gather(bf16[1,1,12]{2,1,0:T(2,128)(2,1)S(1)} %bitcast.96), channel_id=1, replica_groups=mesh['seq'=64,'tp'=4] {'seq'}, dimensions={0}, use_global_device_ids=true | all-gather | bytes 1560 | tf_op jit(solution)/shard_map/all_gather | solution.py:19
  182.2 3.6 fusion.14
  185.8 43.4 %all-gather.14.cloned.1.call-done = bf16[768,64,128]{2,1,0:T(8,128)(2,1)} async-done(((bf16[12,64,128]{2,1,0:T(8,128)(2,1)}), bf16[768,64,128]{2,1,0:T(8,128)(2,1)}) %all-gather.14.cloned.1.call-update) | async-done | bytes 12582928 | tf_op jit(solution)/shard_map/all_gather | solution.py:19
  229.1 70.1 %while.14 = (s32[]{:T(128)}, f32[12,64,128]{2,1,0:T(8,128)S(1)}, s32[]{:T(128)}, bf16[64,12]{1,0:T(8,128)(2,1)S(1)}, bf16[64,12,64,128]{3,2,1,0:T(8,128)(2,1)}, /*index=5*/s32[]{:T(128)}, s32[]{:T(128)}) while((s32[]{:T(128)}, f32[12,64,128]{2,1,0:T(8,128)S(1)}, s32[]{:T(128)}, bf16[64,12]{1,0:T(8,128)(2,1)S(1)}, ...), condition=%wide.region_7.8_spmd.clone, body=%wide.region_6.7_spmd.clone.sunk | while | flops 491536 | bytes 983265 | solution.py:32
  278.4 1.1 fusion.58
  283.9 1.1 fusion.58
  299.3 1.6 fusion.18
  301.2 5.5 %all-gather.10.cloned.1.call-done = bf16[1536,768]{1,0:T(8,128)(2,1)} async-done(((bf16[24,768]{1,0:T(8,128)(2,1)}), bf16[1536,768]{1,0:T(8,128)(2,1)}) %all-gather.10.cloned.1.call-update) | async-done | bytes 2359312 | tf_op jit(solution)/shard_map/all_gather | solution.py:98
  306.7 2.7 multiply_reduce_fusion
  309.4 10.5 %psum.7 = f32[256]{0:T(256)S(1)} all-reduce(f32[256]{0:T(256)S(1)} %get-tuple-element.160), channel_id=1, replica_groups=mesh['seq'=64,'tp'=4] {'tp'}, use_global_device_ids=true, to_apply=%region_9.10 | all-reduce | flops 256 | bytes 2048 | tf_op jit(solution)/shard_map/psum | solution.py:161
  319.8 64.6 %all-gather.12.cloned.1.call-done = bf16[768,1536]{0,1:T(8,128)(2,1)} async-done(((bf16[768,24]{0,1:T(8,128)(2,1)}), bf16[768,1536]{0,1:T(8,128)(2,1)}) %all-gather.12.cloned.1.call-update) | async-done | bytes 2359312 | tf_op jit(solution)/shard_map/all_gather | solution.py:169
  384.4 2.5 convolution_convert_fusion
  386.9 1.2 copy.50
  388.1 23.7 %reduce-scatter.4.cloned.1.call-done = bf16[384,256]{1,0:T(8,128)(2,1)} async-done(((bf16[1536,256]{1,0:T(8,128)(2,1)}), bf16[384,256]{1,0:T(8,128)(2,1)}) %reduce-scatter.4.cloned.1.call-update) | async-done | bytes 196624
  411.8 1.7 copy.51
  (204 shorter events, 79.5 us)
Async XLA Ops:
  6.5 123.6 %all-gather.8.cloned.1.call-start = ((), (), s32[]{:S(2)}) async-start(), calls=%async_computation.1 | async-start | bytes 2396160 | tf_op jit(solution)/shard_map/all_gather | solution.py:99
  8.1 221.1 %all-gather.14.cloned.1.call-start = ((), (), s32[]{:S(2)}) async-start(), calls=%async_computation.4 | async-start | bytes 12779520 | tf_op jit(solution)/shard_map/all_gather | solution.py:19
  75.6 0.9 copy-start.5
  76.2 3.6 copy-start.2
  76.2 3.6 copy-start.4
  132.6 7.1 %collective-permute-start = (bf16[3,1024]{1,0:T(4,128)(2,1)S(1)}, bf16[3,1024]{1,0:T(4,128)(2,1)S(1)}, u32[]{:S(2)}, u32[]{:S(2)}) collective-permute-start(bf16[3,1024]{1,0:T(4,128)(2,1)S(1)} %fusion.40), channel_id=1, source_target_pairs={{0,4},{4,8},{8,12},{12,16},{16,20},{20,24},{24,28},{28,32},{32,36}... | collective-permute-start | bytes 18440 | tf_op jit(solution)/shard_map/ppermute | solution.py:13
  139.9 2.3 copy-start
  139.9 3.1 copy-start.1
  142.2 164.5 %all-gather.10.cloned.1.call-start = ((), (), s32[]{:S(2)}) async-start(), calls=%async_computation.2 | async-start | bytes 2396160 | tf_op jit(solution)/shard_map/all_gather | solution.py:98
  142.9 241.5 %all-gather.12.cloned.1.call-start = ((), (), s32[]{:S(2)}) async-start(), calls=%async_computation.3 | async-start | bytes 2396160 | tf_op jit(solution)/shard_map/all_gather | solution.py:169
  143.6 268.2 %reduce-scatter.4.cloned.1.call-start = ((), (), s32[]{:S(2)}) async-start(), calls=%async_computation.5 | async-start | bytes 983040
  229.1 70.1 %copy-start.6 = (f32[12]{0:T(128)S(1)}, f32[12]{0:T(128)}, u32[]{:S(2)}) copy-start(f32[12]{0:T(128)} %param.25) | copy-start | bytes 148
  301.2 83.2 %copy-start.3 = (f32[768]{0:T(1024)S(1)}, f32[768]{0:T(1024)}, u32[]{:S(2)}) copy-start(f32[768]{0:T(1024)} %param.26) | copy-start | bytes 9220
Sparse Core Ops, SparseCore 0:
  10.1 79.4 all-gather.7
  142.3 86.8 all-gather.13
  231.8 74.7 all-gather.9
  309.2 75.1 all-gather.11
  388.2 23.5 reduce-scatter.3
where the time goes:
time: 422 us; the launch traced here: 420 us
  blocking collectives  158 us (37%)
  waiting for transfers between devices  142 us (34%)
  other arithmetic  79 us (19%)
  matrix products  14.9 us (4%)
  between operations  14.6 us (3%)
  local copies, waits for them, and re-layouts  7.21 us (2%)
    select_n x64, other arithmetic, turn(): return jax.tree.map(lambda a, b: jnp.where(reached, a, b), new, before)  67.4 us
    all_gather x1, waiting for transfers between devices, on_device(): lax.all_gather(out_weight, 'seq', axis=1, tiled=True)  64.6 us
    all_gather x1, blocking collectives, on_device(): lax.all_gather(stored[2], 'seq', axis=0, tiled=True)  48.3 us
    all_gather x1, blocking collectives, on_device(): lax.all_gather(stored[3], 'seq', axis=0, tiled=True)  46.7 us
    all_gather x1, waiting for transfers between devices, prefix_2(): lax.all_gather(part.astype(kind), axis)  43.4 us
    all_gather x1, blocking collectives, prefix_2(): lax.all_gather(part.astype(kind), axis)  38.1 us
    unnamed x6, waiting for transfers between devices  23.8 us
    all_gather x1, blocking collectives, on_device(): gathered = lax.all_gather(hidden_in, 'tp', axis=1, tiled=True)  14.2 us
  transfers between devices with their start and end apart: 6, of which 5 were waited for; matrix products, arithmetic and copies ran while one was open for 21% of the time, Pallas kernels for 0%

commit v1 on v0

--- a/solution.py
+++ b/solution.py
@@ -5,6 +5,22 @@
 
 EPSILON = 1e-05
 HIGHEST_PREC = lax.Precision.HIGHEST
+
+
+def ring_gather(x, axis, dim):
+    ways, here, turn = (lax.axis_size(axis), lax.axis_index(axis), x.shape[dim])
+    lengths = [n * ways if d == dim else n for d, n in enumerate(x.shape)]
+    full = lax.dynamic_update_slice_in_dim(jnp.zeros(lengths, x.dtype), x, here * turn, axis=dim)
+    going_up = going_down = x
+    for far in range(1, ways // 2 + 1):
+        going_up = lax.ppermute(going_up, axis, [(d, (d + 1) % ways) for d in range(ways)])
+        full = lax.dynamic_update_slice_in_dim(full, going_up, (here - far) % ways * turn, axis=dim)
+        if 2 * far < ways:
+            going_down = lax.ppermute(going_down, axis, [(d, (d - 1) % ways) for d in range(ways)])
+            full = lax.dynamic_update_slice_in_dim(
+                full, going_down, (here + far) % ways * turn, axis=dim
+            )
+    return full
 
 
 def passed_along(block, axis, distance):
@@ -82,7 +98,7 @@
     seq_count = lax.axis_size("seq")
     tokens_here = hidden_in.shape[0]
     edge_count = conv_value.shape[0] - 1
-    gathered = lax.all_gather(hidden_in, "tp", axis=1, tiled=True)
+    gathered = ring_gather(hidden_in, "tp", 1)
     row_count = gathered.shape[0]
     model_width = gathered.shape[1]
     permuted = jnp.take(

time: 422 us -> 418 us (level)
  blocking collectives: 158 us -> 143 us
  waiting for transfers between devices: 142 us -> 148 us
    all_gather x1 -> x0, blocking collectives: 14.2 us -> none  [on_device(): gathered = lax.all_gather(hidden_in, 'tp', axis=1, tiled=True)]
    ppermute x0 -> x3, waiting for transfers between devices: none -> 7.96 us  [the longest x2 7.95 us: ring_gather(): lax.ppermute(going_up, axis, [(d, (d + 1) % ways) for d in range(ways)])]
  transfers between devices with their start and end apart: 6 -> 9, of which waited for: 5 -> 6; matrix products, arithmetic and copies ran while one was open for 21% -> 22% of each run, Pallas kernels for 0% -> 0%
where the time goes in v1:
time: 418 us; the launch traced here: 416 us
  waiting for transfers between devices  148 us (35%)
  blocking collectives  143 us (34%)
  other arithmetic  78.4 us (19%)
  matrix products  14.9 us (4%)
  between operations  14.7 us (4%)
  local copies, waits for them, and re-layouts  8.74 us (2%)
  starting transfers between devices  5.84 us (1%)
    select_n x64, other arithmetic, turn(): return jax.tree.map(lambda a, b: jnp.where(reached, a, b), new, before)  67.5 us
    all_gather x1, waiting for transfers between devices, on_device(): lax.all_gather(out_weight, 'seq', axis=1, tiled=True)  64.6 us
    all_gather x1, blocking collectives, on_device(): lax.all_gather(stored[2], 'seq', axis=0, tiled=True)  48.3 us
    all_gather x1, blocking collectives, on_device(): lax.all_gather(stored[3], 'seq', axis=0, tiled=True)  46.8 us
    all_gather x1, waiting for transfers between devices, prefix_2(): lax.all_gather(part.astype(kind), axis)  40.9 us
    all_gather x1, blocking collectives, prefix_2(): lax.all_gather(part.astype(kind), axis)  37.9 us
    unnamed x6, waiting for transfers between devices  23.9 us
    psum x1, blocking collectives, on_device(): square_total = lax.psum(squares, 'tp')  10.5 us
  transfers between devices with their start and end apart: 9, of which 6 were waited for; matrix products, arithmetic and copies ran while one was open for 22% of the time, Pallas kernels for 0%

profile of v1, /device:TPU:2, one launch (start us, length us, event | category | flops | bytes accessed | tf_op | source)
XLA Modules:
  0.0 415.8 jit_solution(4783606770137094219)
XLA Ops:
  6.5 1.5 convert_element_type.112
  9.2 1.7 collective-permute-start
  10.8 1.7 collective-permute-start.1
  14.1 46.8 %all-gather.1 = bf16[64,24,12]{1,2,0:T(8,128)(2,1)S(1)} all-gather(bf16[1,24,12]{1,2,0:T(8,128)(2,1)S(1)} %convert_bitcast_fusion), channel_id=1, replica_groups=mesh['seq'=64,'tp'=4] {'seq'}, dimensions={0}, use_global_device_ids=true | all-gather | bytes 37440 | tf_op jit(solution)/shard_map/all_gather | solution.py:117
  67.5 48.3 %all_gather.26 = bf16[1536,256]{1,0:T(8,128)(2,1)S(1)} all-gather(bf16[24,256]{1,0:T(8,128)(2,1)S(1)} %convert_element_type.114), channel_id=1, replica_groups=mesh['seq'=64,'tp'=4] {'seq'}, dimensions={0}, use_global_device_ids=true | all-gather | bytes 798720 | tf_op jit(solution)/shard_map/all_gather | solution.py:116
  115.8 1.3 broadcast_compare_fusion
  117.7 8.0 %collective-permute-done.2 = bf16[256,384]{0,1:T(8,128)(2,1)S(1)} collective-permute-done((bf16[256,384]{0,1:T(8,128)(2,1)S(1)}, bf16[256,384]{0,1:T(8,128)(2,1)S(1)}, u32[]{:S(2)}, u32[]{:S(2)}) %collective-permute-start.2) | collective-permute-done | bytes 196640 | tf_op jit(solution)/shard_map/ppermute | solution.py:16
  128.5 2.5 convolution_convert_fusion.2
  131.0 1.9 collective-permute-start.3
  132.9 5.1 %collective-permute-done.3 = bf16[3,1024]{1,0:T(4,128)(2,1)S(1)} collective-permute-done((bf16[3,1024]{1,0:T(4,128)(2,1)S(1)}, bf16[3,1024]{1,0:T(4,128)(2,1)S(1)}, u32[]{:S(2)}, u32[]{:S(2)}) %collective-permute-start.3) | collective-permute-done | bytes 6176 | tf_op jit(solution)/shard_map/ppermute | solution.py:29
  139.3 1.2 fusion.20
  142.3 37.9 %all-gather.2 = bf16[64,1,12]{2,1,0:T(2,128)(2,1)S(1)} all-gather(bf16[1,1,12]{2,1,0:T(2,128)(2,1)S(1)} %bitcast.96), channel_id=1, replica_groups=mesh['seq'=64,'tp'=4] {'seq'}, dimensions={0}, use_global_device_ids=true | all-gather | bytes 1560 | tf_op jit(solution)/shard_map/all_gather | solution.py:35
  180.4 3.6 fusion.14
  184.0 40.9 %all-gather.14.cloned.1.call-done = bf16[768,64,128]{2,1,0:T(8,128)(2,1)} async-done(((bf16[12,64,128]{2,1,0:T(8,128)(2,1)}), bf16[768,64,128]{2,1,0:T(8,128)(2,1)}) %all-gather.14.cloned.1.call-update) | async-done | bytes 12582928 | tf_op jit(solution)/shard_map/all_gather | solution.py:35
  224.8 70.1 %while.14 = (s32[]{:T(128)}, f32[12,64,128]{2,1,0:T(8,128)S(1)}, s32[]{:T(128)}, bf16[64,12]{1,0:T(8,128)(2,1)S(1)}, bf16[64,12,64,128]{3,2,1,0:T(8,128)(2,1)}, /*index=5*/s32[]{:T(128)}, s32[]{:T(128)}) while((s32[]{:T(128)}, f32[12,64,128]{2,1,0:T(8,128)S(1)}, s32[]{:T(128)}, bf16[64,12]{1,0:T(8,128)(2,1)S(1)}, ...), condition=%wide.region_7.8_spmd.clone, body=%wide.region_6.7_spmd.clone.sunk | while | flops 491536 | bytes 983265 | solution.py:48
  294.9 1.6 fusion.18
  296.9 5.5 %all-gather.10.cloned.1.call-done = bf16[1536,768]{1,0:T(8,128)(2,1)} async-done(((bf16[24,768]{1,0:T(8,128)(2,1)}), bf16[1536,768]{1,0:T(8,128)(2,1)}) %all-gather.10.cloned.1.call-update) | async-done | bytes 2359312 | tf_op jit(solution)/shard_map/all_gather | solution.py:114
  302.4 2.7 multiply_reduce_fusion
  305.0 10.5 %psum.7 = f32[256]{0:T(256)S(1)} all-reduce(f32[256]{0:T(256)S(1)} %get-tuple-element.160), channel_id=1, replica_groups=mesh['seq'=64,'tp'=4] {'tp'}, use_global_device_ids=true, to_apply=%region_9.10 | all-reduce | flops 256 | bytes 2048 | tf_op jit(solution)/shard_map/psum | solution.py:177
  315.5 64.6 %all-gather.12.cloned.1.call-done = bf16[768,1536]{0,1:T(8,128)(2,1)} async-done(((bf16[768,24]{0,1:T(8,128)(2,1)}), bf16[768,1536]{0,1:T(8,128)(2,1)}) %all-gather.12.cloned.1.call-update) | async-done | bytes 2359312 | tf_op jit(solution)/shard_map/all_gather | solution.py:185
  380.1 2.5 convolution_convert_fusion
  382.6 1.2 copy.56
  383.8 23.8 %reduce-scatter.4.cloned.1.call-done = bf16[384,256]{1,0:T(8,128)(2,1)} async-done(((bf16[1536,256]{1,0:T(8,128)(2,1)}), bf16[384,256]{1,0:T(8,128)(2,1)}) %reduce-scatter.4.cloned.1.call-update) | async-done | bytes 196624
  407.5 1.7 copy.57
  (212 shorter events, 83.0 us)
Async XLA Ops:
  6.5 109.3 %copy-start.5 = (s32[64]{0:T(128)S(1)}, s32[64]{0:T(128)}, u32[]{:S(2)}) copy-start(s32[64]{0:T(128)} %param.29) | copy-start | bytes 772
  6.5 121.9 %all-gather.8.cloned.1.call-start = ((), (), s32[]{:S(2)}) async-start(), calls=%async_computation.1 | async-start | bytes 2396160 | tf_op jit(solution)/shard_map/all_gather | solution.py:115
  8.1 216.8 %all-gather.14.cloned.1.call-start = ((), (), s32[]{:S(2)}) async-start(), calls=%async_computation.4 | async-start | bytes 12779520 | tf_op jit(solution)/shard_map/all_gather | solution.py:35
  9.2 108.0 %collective-permute-start = (bf16[256,384]{0,1:T(8,128)(2,1)S(1)}, bf16[256,384]{0,1:T(8,128)(2,1)S(1)}, u32[]{:S(2)}, u32[]{:S(2)}) collective-permute-start(bf16[256,384]{0,1:T(8,128)(2,1)S(1)} %copy.43), channel_id=1, source_target_pairs={{0,1},{1,2},{2,3},{3,0},{4,5},{5,6},{6,7},{7,4},{8,9},{9,10},{10,1... | collective-permute-start | bytes 589832 | tf_op jit(solution)/shard_map/ppermute | solution.py:16
  10.8 106.8 %collective-permute-start.1 = (bf16[256,384]{0,1:T(8,128)(2,1)S(1)}, bf16[256,384]{0,1:T(8,128)(2,1)S(1)}, u32[]{:S(2)}, u32[]{:S(2)}) collective-permute-start(bf16[256,384]{0,1:T(8,128)(2,1)S(1)} %copy.43), channel_id=1, source_target_pairs={{0,3},{1,0},{2,1},{3,2},{4,7},{5,4},{6,5},{7,6},{8,11},{9,8},{10,9... | collective-permute-start | bytes 589832 | tf_op jit(solution)/shard_map/ppermute | solution.py:19
  117.2 8.4 %collective-permute-start.2 = (bf16[256,384]{0,1:T(8,128)(2,1)S(1)}, bf16[256,384]{0,1:T(8,128)(2,1)S(1)}, u32[]{:S(2)}, u32[]{:S(2)}) collective-permute-start(bf16[256,384]{0,1:T(8,128)(2,1)S(1)} %collective-permute-done), channel_id=1, source_target_pairs={{0,1},{1,2},{2,3},{3,0},{4,5},{5,6},{6,7},{7,4},{8,9},{9,10},{10,1... | collective-permute-start | bytes 589832 | tf_op jit(solution)/shard_map/ppermute | solution.py:16
  125.7 0.9 copy-start.3
  131.0 7.1 %collective-permute-start.3 = (bf16[3,1024]{1,0:T(4,128)(2,1)S(1)}, bf16[3,1024]{1,0:T(4,128)(2,1)S(1)}, u32[]{:S(2)}, u32[]{:S(2)}) collective-permute-start(bf16[3,1024]{1,0:T(4,128)(2,1)S(1)} %fusion.40), channel_id=1, source_target_pairs={{0,4},{4,8},{8,12},{12,16},{16,20},{20,24},{24,28},{28,32},{32,36}... | collective-permute-start | bytes 18440 | tf_op jit(solution)/shard_map/ppermute | solution.py:29
  138.2 2.3 copy-start
  138.2 3.1 copy-start.1
  140.5 161.9 %all-gather.10.cloned.1.call-start = ((), (), s32[]{:S(2)}) async-start(), calls=%async_computation.2 | async-start | bytes 2396160 | tf_op jit(solution)/shard_map/all_gather | solution.py:114
  141.2 238.9 %all-gather.12.cloned.1.call-start = ((), (), s32[]{:S(2)}) async-start(), calls=%async_computation.3 | async-start | bytes 2396160 | tf_op jit(solution)/shard_map/all_gather | solution.py:185
  141.9 265.6 %reduce-scatter.4.cloned.1.call-start = ((), (), s32[]{:S(2)}) async-start(), calls=%async_computation.5 | async-start | bytes 983040
  224.8 70.1 %copy-start.4 = (f32[12]{0:T(128)S(1)}, f32[12]{0:T(128)}, u32[]{:S(2)}) copy-start(f32[12]{0:T(128)} %param.25) | copy-start | bytes 148
  296.9 83.2 %copy-start.2 = (f32[768]{0:T(1024)S(1)}, f32[768]{0:T(1024)}, u32[]{:S(2)}) copy-start(f32[768]{0:T(1024)} %param.26) | copy-start | bytes 9220
Sparse Core Ops, SparseCore 0:
  10.1 79.5 all-gather.7
  140.6 84.1 all-gather.13
  227.5 74.7 all-gather.9
  304.9 75.1 all-gather.11
  383.9 23.5 reduce-scatter.3
